TPU v7x, 32 devices: a whole 2x2x4 slice. The times are simulated.
32 devices in a mesh: cell: 2 (over x), ap: 8 (over z, y), sc: 2 (over core).
Axes of the slice: x: 2, y: 2, z: 4, core: 2. Of those that a mesh axis runs over, the one named last changes fastest.
Arguments:
- unsmoothed_link_guesses: bfloat16 [32, 4, 2, 128, 2048], P(('cell', 'ap'), None, None, None, 'sc'), parts along dimension 0, may hold values from -24 to 24
- received: bfloat16 [32, 4, 2, 4, 2048], P(('cell', 'ap'), None, None, None, 'sc'), parts along dimension 0, may hold values from -6 to 6
- user_power: float32 [256], P('cell'), parts along dimension 0, may hold values from 0.25 to 4
- noise_power: float32 [32], P(('cell', 'ap')), parts along dimension 0, may hold values from 0.1 to 1
- ap_gain: float32 [32, 128], P(('cell', 'ap')), parts along dimension 0, may hold values from 0.5 to 4
- user_cluster: int32 [256], P('cell'), parts along dimension 0, may hold values from 0 to 15, as said below
- serving: int32 [32, 16], P('cell'), parts along dimension 0, may hold values from 0 to 1, as said below
- cluster_owner: int32 [32, 1], P('cell'), parts along dimension 0, may hold values from 0 to 7, as said below
Outputs:
- estimates: float32 [64, 8, 4, 2, 2048], P(('cell', 'ap'), None, None, None, 'sc'), parts along dimension 0
There are 2 independent parts, one for each index of `cell`. A program takes and returns all parts, laid end to end along the dimension named above; each array names one. Nothing has to cross between parts.
Inputs may be any that keep to these rules, and one draw needn't show every extreme that they name: `user_cluster`: each of the 16 clusters holds exactly 8 users. `serving`: column a belongs to index a // 2 of ap. Where a cluster is served by an index of ap, at least one of its access points serves it. Of the clusters that one index of ap serves, at most 2 have the same owner; in every draw some owner has exactly 2 of its clusters served by every index of ap. `cluster_owner`: at most 4 clusters have the same owner, and some owner has exactly 4.
All inputs are finite; a program needn't handle non-finite values.
Results may differ from a plain program's by a relative error of at most 0.017.
Values may be sent and summed in bfloat16 or wider, within the bound.
A program may use at most 128 MiB of HBM per device.

v0:
```python
import math
import jax
import jax.numpy as jnp
from jax import lax
from jax.sharding import PartitionSpec as P

TONE_NUMBER = 2048
TAPS = 64
CU = 8
OWN_MAX = 4


def complex_times(left_factor, right_factor):
    return (
        left_factor[0] * right_factor[0] - left_factor[1] * right_factor[1],
        left_factor[0] * right_factor[1] + left_factor[1] * right_factor[0],
    )


def times_conj(left_factor, right_factor):
    return (
        left_factor[0] * right_factor[0] + left_factor[1] * right_factor[1],
        left_factor[1] * right_factor[0] - left_factor[0] * right_factor[1],
    )


def hermitian_solve(cov_re, cov_im, right_re, right_im):
    dimension = len(cov_re)
    factor = {}
    pivots = []
    for j in range(dimension):
        pivot_root = cov_re[j][j]
        for k in range(j):
            element = factor[j, k]
            pivot_root = pivot_root - (element[0] * element[0] + element[1] * element[1])
        pivot_root = jnp.sqrt(pivot_root)
        pivots.append(pivot_root)
        for i in range(j + 1, dimension):
            running = (cov_re[i][j], cov_im[i][j])
            for k in range(j):
                product = times_conj(factor[i, k], factor[j, k])
                running = (running[0] - product[0], running[1] - product[1])
            factor[i, j] = (running[0] / pivot_root, running[1] / pivot_root)
    forward = []
    for i in range(dimension):
        running = (right_re[i], right_im[i])
        for k in range(i):
            product = complex_times(factor[i, k], forward[k])
            running = (running[0] - product[0], running[1] - product[1])
        forward.append((running[0] / pivots[i], running[1] / pivots[i]))
    result = [None] * dimension
    for i in range(dimension - 1, -1, -1):
        running = forward[i]
        for k in range(i + 1, dimension):
            product = times_conj(result[k], factor[k, i])
            running = (running[0] - product[0], running[1] - product[1])
        result[i] = (running[0] / pivots[i], running[1] / pivots[i])
    return result


def tone_angles(lowest_tone, tone_quantity, tones_first):
    if tones_first:
        tone_values = lowest_tone + lax.broadcasted_iota(jnp.int32, (tone_quantity, TAPS), 0)
        lag_values = lax.broadcasted_iota(jnp.int32, (tone_quantity, TAPS), 1)
    else:
        tone_values = lowest_tone + lax.broadcasted_iota(jnp.int32, (TAPS, tone_quantity), 1)
        lag_values = lax.broadcasted_iota(jnp.int32, (TAPS, tone_quantity), 0)
    rotation = tone_values * lag_values % TONE_NUMBER
    return rotation.astype(jnp.float32) * (2.0 * math.pi / TONE_NUMBER)


def forward_table(lowest_tone, tone_quantity):
    angles = tone_angles(lowest_tone, tone_quantity, True)
    return jnp.concatenate([jnp.cos(angles), jnp.sin(angles)], axis=1).astype(jnp.bfloat16)


def rebuild_tables(lowest_tone, tone_quantity):
    angles = tone_angles(lowest_tone, tone_quantity, False)
    cosine = jnp.cos(angles).astype(jnp.bfloat16)
    sine = jnp.sin(angles).astype(jnp.bfloat16)
    return (jnp.concatenate([cosine, sine], axis=0), jnp.concatenate([-sine, cosine], axis=0))


def rotate_matrix():
    rows = lax.broadcasted_iota(jnp.int32, (2 * TAPS, 2 * TAPS), 0)
    cols = lax.broadcasted_iota(jnp.int32, (2 * TAPS, 2 * TAPS), 1)
    lower = jnp.where((cols < TAPS) & (rows == cols + TAPS), -1.0, 0.0)
    upper = jnp.where((cols >= TAPS) & (rows == cols - TAPS), 1.0, 0.0)
    return (lower + upper).astype(jnp.float32)


def local_estimates(smooth_re, smooth_im, power_row, noise_level, right_side, weight_row):
    antennas = smooth_re.shape[0]
    user_scale = (power_row / smooth_re.shape[1])[:, None]
    scaled_re = [smooth_re[i] * user_scale for i in range(antennas)]
    scaled_im = [smooth_im[i] * user_scale for i in range(antennas)]
    cov_re = [[None] * antennas for i in range(antennas)]
    cov_im = [[None] * antennas for i in range(antennas)]
    for i in range(antennas):
        for j in range(i + 1):
            cov_re[i][j] = jnp.sum(
                scaled_re[i] * smooth_re[j] + scaled_im[i] * smooth_im[j], axis=0
            )
            if i == j:
                cov_re[i][j] = cov_re[i][j] + noise_level
            else:
                cov_im[i][j] = jnp.sum(
                    scaled_im[i] * smooth_re[j] - scaled_re[i] * smooth_im[j], axis=0
                )
    signal = right_side.astype(jnp.float32)
    solved = hermitian_solve(cov_re, cov_im, signal[:, 0], signal[:, 1])
    est_re = (
        smooth_re[0][:, None, :] * solved[0][0][None]
        + smooth_im[0][:, None, :] * solved[0][1][None]
    )
    est_im = (
        smooth_re[0][:, None, :] * solved[0][1][None]
        - smooth_im[0][:, None, :] * solved[0][0][None]
    )
    for i in range(1, antennas):
        est_re = (
            est_re
            + smooth_re[i][:, None, :] * solved[i][0][None]
            + smooth_im[i][:, None, :] * solved[i][1][None]
        )
        est_im = (
            est_im
            + smooth_re[i][:, None, :] * solved[i][1][None]
            - smooth_im[i][:, None, :] * solved[i][0][None]
        )
    return weight_row[:, None, None, None] * jnp.stack([est_re, est_im], axis=2)


def local(
    unsmoothed_link_guesses,
    received,
    user_power,
    noise_power,
    ap_gain,
    user_cluster,
    serving,
    cluster_owner,
):
    ap_count = unsmoothed_link_guesses.shape[0]
    antennas = unsmoothed_link_guesses.shape[1]
    user_count = unsmoothed_link_guesses.shape[3]
    tone_positions = unsmoothed_link_guesses.shape[4]
    clusters = serving.shape[0]
    devices = lax.axis_size("ap")
    device = lax.axis_index("ap")
    lowest_tone = lax.axis_index("sc") * tone_positions
    products = jnp.dot(
        unsmoothed_link_guesses.reshape(-1, tone_positions),
        forward_table(lowest_tone, tone_positions),
        preferred_element_type=jnp.float32,
    )
    products = products.reshape((ap_count, antennas, 2, user_count, 2 * TAPS))
    rotated = jnp.dot(
        products[:, :, 1].reshape(-1, 2 * TAPS), rotate_matrix(), precision=lax.Precision.HIGHEST
    )
    combined = (
        products[:, :, 0] + rotated.reshape((ap_count, antennas, user_count, 2 * TAPS))
    ) / TONE_NUMBER
    coefficients = lax.psum(combined.astype(jnp.bfloat16), "sc")
    coef_b = coefficients.reshape(-1, 2 * TAPS)
    table_re, table_im = rebuild_tables(lowest_tone, tone_positions)
    smooth_re = jnp.dot(coef_b, table_re, preferred_element_type=jnp.float32).reshape(
        (ap_count, antennas, user_count, tone_positions)
    )
    smooth_im = jnp.dot(coef_b, table_im, preferred_element_type=jnp.float32).reshape(
        (ap_count, antennas, user_count, tone_positions)
    )
    cluster_ids = jnp.arange(clusters, dtype=jnp.int32)
    onehot = (user_cluster[:, None] == cluster_ids[None, :]).astype(jnp.float32)
    own_columns = lax.dynamic_slice_in_dim(serving, device * ap_count, ap_count, 1).astype(
        jnp.float32
    )
    weights = jnp.dot(onehot, own_columns, precision=lax.Precision.HIGHEST).T * ap_gain
    totals = lax.psum(jnp.sum(weights, axis=0), "ap")
    partial_value = local_estimates(
        smooth_re[0], smooth_im[0], user_power, noise_power[0], received[0], weights[0]
    )
    partial_value = partial_value + local_estimates(
        smooth_re[1], smooth_im[1], user_power, noise_power[1], received[1], weights[1]
    )
    partial_value = partial_value.astype(jnp.bfloat16)
    owner_map = cluster_owner[:, 0]
    same_owner = owner_map[:, None] == owner_map[None, :]
    earlier = cluster_ids[None, :] < cluster_ids[:, None]
    cluster_rank = jnp.sum(same_owner & earlier, axis=1)
    user_ids = jnp.arange(user_count, dtype=jnp.int32)
    position = jnp.sum(
        (user_cluster[:, None] == user_cluster[None, :]) & (user_ids[None, :] < user_ids[:, None]),
        axis=1,
    )
    member_hits = (user_cluster[None, None, :] == cluster_ids[:, None, None]) & (
        position[None, None, :] == jnp.arange(CU, dtype=jnp.int32)[None, :, None]
    )
    members = jnp.sum(jnp.where(member_hits, user_ids[None, None, :], 0), axis=2)
    slot_ids = jnp.arange(devices * OWN_MAX, dtype=jnp.int32)
    slot_hits = (owner_map[None, :] == (slot_ids // OWN_MAX)[:, None]) & (
        cluster_rank[None, :] == (slot_ids % OWN_MAX)[:, None]
    )
    hit_table = slot_hits.astype(jnp.int32)
    filled = jnp.sum(hit_table, axis=1)
    member_rows = jnp.sum(hit_table[:, :, None] * members[None], axis=1)
    picked = jnp.take(partial_value, member_rows.reshape(-1), axis=0)
    picked = picked.reshape(member_rows.shape + partial_value.shape[1:])
    owner_sums = lax.psum_scatter(
        picked * filled.astype(jnp.bfloat16)[:, None, None, None, None],
        "ap",
        scatter_dimension=0,
        tiled=True,
    ).astype(jnp.float32)
    my_hits = (
        (owner_map[None, :] == device)
        & (cluster_rank[None, :] == jnp.arange(OWN_MAX, dtype=jnp.int32)[:, None])
    ).astype(jnp.int32)
    my_rows = jnp.sum(my_hits[:, :, None] * members[None], axis=1)
    my_filled = jnp.sum(my_hits, axis=1).astype(jnp.float32)
    denominator = (
        1.0 + jnp.take(totals, my_rows.reshape(-1)).reshape(my_rows.shape) * my_filled[:, None]
    )
    return owner_sums / denominator[:, :, None, None, None]


def solution(mesh):
    placed = (
        P(("cell", "ap"), None, None, None, "sc"),
        P(("cell", "ap"), None, None, None, "sc"),
        P("cell"),
        P(("cell", "ap")),
        P(("cell", "ap"), None),
        P("cell"),
        P("cell", None),
        P("cell", None),
    )
    return jax.shard_map(
        local,
        mesh=mesh,
        in_specs=placed,
        out_specs=P(("cell", "ap"), None, None, None, "sc"),
        check_vma=False,
    )
```

profile of v0, /device:TPU:0, one launch (start us, length us, event | category | flops | bytes accessed | tf_op | source)
XLA Modules:
  0.0 179.8 jit_solution(7883190322390066773)
XLA Ops:
  6.6 2.5 %cosine_convert_fusion = (bf16[1024,64]{1,0:T(8,128)(2,1)S(1)}, bf16[1024,64]{1,0:T(8,128)(2,1)S(1)}) fusion(s32[1024]{0:T(1024)S(1)} %iota_add_fusion), kind=kLoop, calls=%fused_computation.154 | loop fusion | flops 1048576 | bytes 266240 | tf_op jit(solution)/shard_map/convert.2
  9.1 3.9 %convolution_bitcast_fusion = f32[2048,128]{0,1:T(8,128)S(1)} fusion(bf16[2048,1024]{1,0:T(8,128)(2,1)} %bitcast.232, bf16[1024,64]{1,0:T(8,128)(2,1)S(1)} %get-tuple-element.144, bf16[1024,64]{1,0:T(8,128)(2,1)S(1)} %get-tuple-element.143), kind=kOutput, calls=%fused_computation.8 | convolution fusion | flops 537395200 | bytes 5505024 | tf_op jit(solution)/shard_map/dot_general | solution.py:152
  13.0 0.9 reshape.10782
  13.9 0.8 fusion.186
  15.6 1.3 fusion.4
  17.1 1.1 sine_convert_fusion.1
  18.2 1.0 fusion.110
  21.6 16.4 %all-reduce.2.cloned.1.call-done = bf16[1024,128]{1,0:T(8,128)(2,1)} async-done(((bf16[1024,128]{1,0:T(8,128)(2,1)}), bf16[1024,128]{1,0:T(8,128)(2,1)}) %all-reduce.2.cloned.1.call-update) | async-done | bytes 262160 | tf_op jit(solution)/shard_map/psum | solution.py:164
  38.0 1.7 fusion.82
  40.4 1.1 fusion.50
  41.6 0.9 fusion.28
  42.4 0.9 fusion.24
  43.3 0.9 fusion.22
  44.2 1.0 fusion.32
  50.4 4.1 %multiply_add_fusion = (f32[128,4,1,1024]{3,1,2,0:T(4,128)S(1)}, f32[128,4,1,1024]{3,1,2,0:T(4,128)S(1)}) fusion(f32[4,1024]{1,0:T(4,128)S(1)} %get-tuple-element.42, f32[128,1024]{1,0:T(8,128)S(1)} %get-tuple-element.103, f32[4,1024]{1,0:T(4,128)S(1)} %get-tuple-element.41, f32[128,1024]{1,0:T(8,128)S(1)} %get-tuple-element.109, ...), kind=kLoop, calls=%fused_computation.10 | loop fusion | flops 15728640 | bytes 8519680 | tf_op jit(solution)/shard_map/add | solution.py:122
  54.6 4.2 %multiply_add_fusion.1 = (f32[128,4,1,1024]{3,1,2,0:T(4,128)S(1)}, f32[128,4,1,1024]{3,1,2,0:T(4,128)S(1)}) fusion(f32[4,1024]{1,0:T(4,128)S(1)} %get-tuple-element.71, f32[128,1024]{1,0:T(8,128)S(1)} %get-tuple-element.112, f32[4,1024]{1,0:T(4,128)S(1)} %get-tuple-element.70, f32[128,1024]{1,0:T(8,128)S(1)} %get-tuple-element.114, ...), kind=kLoop, calls=%fused_computation.12 | loop fusion | flops 15728640 | bytes 8519680 | tf_op jit(solution)/shard_map/add | solution.py:122
  58.7 2.1 %fusion.1 = bf16[128,4,2,1024]{3,1,2,0:T(4,128)(2,1)S(1)} fusion(f32[128,4,1,1024]{3,1,2,0:T(4,128)S(1)} %get-tuple-element.98, f32[128,4,1,1024]{3,1,2,0:T(4,128)S(1)} %get-tuple-element.97, f32[128,4,1,1024]{3,1,2,0:T(4,128)S(1)} %get-tuple-element.96, f32[128,4,1,1024]{3,1,2,0:T(4,128)S(1)} %get-tuple-element.95, f32[128]{0:T(128)S(1)} %get-tuple-element.146, ...), kind=kLoop, calls=%fused_computation.4 | loop fusion | flops 6291456 | bytes 10486784 | tf_op jit(solution)/shard_map/convert_element_type | solution.py:186
  60.8 9.8 %gather_fusion = bf16[256,4,2,1024]{3,1,2,0:T(4,128)(2,1)} fusion(bf16[128,4,2,1024]{3,1,2,0:T(4,128)(2,1)S(1)} %fusion.1, s32[1024]{0:T(1024)S(1)} %pad_clamp_fusion.1), kind=kCustom, calls=%fused_computation | custom fusion | bytes 8389632 | tf_op jit(solution)/shard_map/jit(_take)/gather | solution.py:207
  70.7 7.1 %fusion.2 = bf16[32,8,4,2,1024]{4,1,0,3,2:T(8,128)(2,1)S(1)} fusion(bf16[256,4,2,1024]{3,1,2,0:T(4,128)(2,1)} %gather_fusion, pred[32,8]{1,0:T(8,128)(4,1)S(1)} %copy.25, bf16[32]{0:T(256)(128)(2,1)S(1)} %convert_element_type.86), kind=kLoop, calls=%fused_computation.7 | loop fusion | flops 4194304 | bytes 8388928 | tf_op jit(solution)/shard_map/mul | solution.py:210
  77.7 2.4 %copy.30 = bf16[32,8,4,2,1024]{4,1,3,2,0:T(8,128)(2,1)} copy(bf16[32,8,4,2,1024]{4,1,0,3,2:T(8,128)(2,1)S(1)} %fusion.2) | data formatting | bytes 8388608 | tf_op jit(solution)/shard_map/mul | solution.py:210
  80.5 21.9 %psum.15 = f32[128]{0:T(128)S(1)} all-reduce(f32[128]{0:T(128)S(1)} %get-tuple-element.149), channel_id=1, replica_groups=mesh['cell'=2,'ap'=8,'sc'=2] {'ap'}, use_global_device_ids=true, to_apply=%region_41.42 | all-reduce | flops 128 | bytes 1024 | tf_op jit(solution)/shard_map/psum | solution.py:179
  103.4 66.6 %reduce-scatter.2.cloned.1.call-done = bf16[4,8,4,2,1024]{4,1,3,2,0:T(8,128)(2,1)} async-done(((bf16[32,8,4,2,1024]{4,1,3,2,0:T(8,128)(2,1)}), bf16[4,8,4,2,1024]{4,1,3,2,0:T(8,128)(2,1)}) %reduce-scatter.2.cloned.1.call-update) | async-done | bytes 524304 | tf_op jit(solution)/shard_map/reduce_scatter | solution.py:209
  170.0 1.2 convert_divide_fusion
  171.2 1.8 copy.32
  (76 shorter events, 10.4 us)
Async XLA Ops:
  6.5 31.5 %all-reduce.2.cloned.1.call-start = ((), (), s32[]{:S(2)}) async-start(), calls=%async_computation.1 | async-start | bytes 524288 | tf_op jit(solution)/shard_map/psum | solution.py:164
  14.7 4.5 %copy-start.4 = (s32[128]{0:T(128)S(1)}, s32[128]{0:T(128)}, u32[]{:S(2)}) copy-start(s32[128]{0:T(128)} %param.13) | copy-start | bytes 1540
  14.7 4.7 %copy-start.2 = (s32[16,1]{0,1:T(1,128)S(1)}, s32[16,1]{0,1:T(1,128)}, u32[]{:S(2)}) copy-start(s32[16,1]{0,1:T(1,128)} %param.15) | copy-start | bytes 196
  14.7 5.6 %copy-start.7 = (f32[128]{0:T(128)S(1)}, f32[128]{0:T(128)}, u32[]{:S(2)}) copy-start(f32[128]{0:T(128)} %param.10) | copy-start | bytes 1540
  14.7 5.6 %copy-start.3 = (f32[2]{0:T(128)S(1)}, f32[2]{0:T(128)}, u32[]{:S(2)}) copy-start(f32[2]{0:T(128)} %param.11) | copy-start | bytes 28
  14.7 6.3 %copy-start.5 = (s32[16,16]{1,0:T(8,128)S(1)}, s32[16,16]{1,0:T(8,128)}, u32[]{:S(2)}) copy-start(s32[16,16]{1,0:T(8,128)} %param.14) | copy-start | bytes 3076
  14.7 6.3 %copy-start.6 = (f32[2,128]{1,0:T(2,128)S(1)}, f32[2,128]{1,0:T(2,128)}, u32[]{:S(2)}) copy-start(f32[2,128]{1,0:T(2,128)} %param.12) | copy-start | bytes 3076
  14.8 6.8 %copy-start.1 = (bf16[2,4,2,4,1024]{4,3,2,1,0:T(4,128)(2,1)S(1)}, bf16[2,4,2,4,1024]{4,3,2,1,0:T(4,128)(2,1)}, u32[]{:S(2)}) copy-start(bf16[2,4,2,4,1024]{4,3,2,1,0:T(4,128)(2,1)} %param.9) | copy-start | bytes 393220
  16.9 153.1 %reduce-scatter.2.cloned.1.call-start = ((), (), s32[]{:S(2)}) async-start(), calls=%async_computation.2 | async-start | bytes 4718592 | tf_op jit(solution)/shard_map/reduce_scatter | solution.py:209
  38.0 1.7 copy-start
Sparse Core Ops, SparseCore 0:
  17.0 20.9 all-reduce.1
  80.3 89.6 reduce-scatter.1
where the time goes:
time: 180 us
  waiting for transfers between devices  83.1 us (46%)
  other arithmetic  34.6 us (19%)
  blocking collectives  21.9 us (12%)
  local copies, waits for them, and re-layouts  18.4 us (10%)
  between operations  13.8 us (8%)
  matrix products  7.85 us (4%)
    reduce_scatter x1, waiting for transfers between devices, local(): lax.psum_scatter(picked * filled.astype(jnp.bfloat16)[:, None, None, None...  66.6 us
    psum x1, blocking collectives, local(): totals = lax.psum(jnp.sum(weights, axis=0), 'ap')  21.9 us
    psum x1, waiting for transfers between devices, local(): coefficients = lax.psum(combined.astype(jnp.bfloat16), 'sc')  16.4 us
    gather x1, local copies, waits for them, and re-layouts, local(): picked = jnp.take(partial_value, member_rows.reshape(-1), axis=0)  9.81 us
    add x2, other arithmetic, local_estimates(): est_re + smooth_re[i][:, None, :] * solved[i][0][None]  8.3 us
    mul x1, other arithmetic, local(): picked * filled.astype(jnp.bfloat16)[:, None, None, None, None]  7.08 us
    dot_general x1, matrix products, local(): jnp.dot(unsmoothed_link_guesses.reshape(-1, tone_positions), forward_tabl...  3.9 us
    another operation x3, other arithmetic  3.78 us
  transfers between devices with their start and end apart: 2, of which 2 were waited for; matrix products, arithmetic and copies ran while one was open for 3% of the time, Pallas kernels for 0%

commit v1 on v0

--- a/solution.py
+++ b/solution.py
@@ -176,7 +176,9 @@
         jnp.float32
     )
     weights = jnp.dot(onehot, own_columns, precision=lax.Precision.HIGHEST).T * ap_gain
-    totals = lax.psum(jnp.sum(weights, axis=0), "ap")
+    part = jnp.sum(weights, axis=0)
+    pieces = lax.all_gather(part, "ap", axis=0, tiled=False)
+    totals = pieces.sum(axis=0)
     partial_value = local_estimates(
         smooth_re[0], smooth_im[0], user_power, noise_power[0], received[0], weights[0]
     )

time: 180 us -> 180 us (level)
    psum x1 -> x0, blocking collectives: 21.9 us -> none  [local(): totals = lax.psum(jnp.sum(weights, axis=0), 'ap')]
    all_gather x0 -> x1, blocking collectives: none -> 21.2 us  [local(): pieces = lax.all_gather(part, 'ap', axis=0, tiled=False)]
where the time goes in v1:
time: 180 us
  waiting for transfers between devices  83.7 us (46%)
  other arithmetic  34.6 us (19%)
  blocking collectives  21.2 us (12%)
  local copies, waits for them, and re-layouts  18.4 us (10%)
  between operations  13.8 us (8%)
  matrix products  7.85 us (4%)
    reduce_scatter x1, waiting for transfers between devices, local(): lax.psum_scatter(picked * filled.astype(jnp.bfloat16)[:, None, None, None...  67.2 us
    all_gather x1, blocking collectives, local(): pieces = lax.all_gather(part, 'ap', axis=0, tiled=False)  21.2 us
    psum x1, waiting for transfers between devices, local(): coefficients = lax.psum(combined.astype(jnp.bfloat16), 'sc')  16.4 us
    gather x1, local copies, waits for them, and re-layouts, local(): picked = jnp.take(partial_value, member_rows.reshape(-1), axis=0)  9.81 us
    add x2, other arithmetic, local_estimates(): est_re + smooth_re[i][:, None, :] * solved[i][0][None]  8.31 us
    mul x1, other arithmetic, local(): picked * filled.astype(jnp.bfloat16)[:, None, None, None, None]  7.08 us
    dot_general x1, matrix products, local(): jnp.dot(unsmoothed_link_guesses.reshape(-1, tone_positions), forward_tabl...  3.9 us
    another operation x3, other arithmetic  3.78 us
  transfers between devices with their start and end apart: 2, of which 2 were waited for; matrix products, arithmetic and copies ran while one was open for 3% of the time, Pallas kernels for 0%

profile of v1, /device:TPU:0, one launch (start us, length us, event | category | flops | bytes accessed | tf_op | source)
XLA Modules:
  0.0 179.7 jit_solution(5470798991702730159)
XLA Ops:
  6.6 2.5 %cosine_convert_fusion = (bf16[1024,64]{1,0:T(8,128)(2,1)S(1)}, bf16[1024,64]{1,0:T(8,128)(2,1)S(1)}) fusion(s32[1024]{0:T(1024)S(1)} %iota_add_fusion), kind=kLoop, calls=%fused_computation.154 | loop fusion | flops 1048576 | bytes 266240 | tf_op jit(solution)/shard_map/convert.2
  9.1 3.9 %convolution_bitcast_fusion = f32[2048,128]{0,1:T(8,128)S(1)} fusion(bf16[2048,1024]{1,0:T(8,128)(2,1)} %bitcast.233, bf16[1024,64]{1,0:T(8,128)(2,1)S(1)} %get-tuple-element.144, bf16[1024,64]{1,0:T(8,128)(2,1)S(1)} %get-tuple-element.143), kind=kOutput, calls=%fused_computation.8 | convolution fusion | flops 537395200 | bytes 5505024 | tf_op jit(solution)/shard_map/dot_general | solution.py:152
  13.0 0.9 reshape.10782
  13.9 0.8 fusion.186
  15.6 1.3 fusion.4
  17.1 1.1 sine_convert_fusion.1
  18.2 1.0 fusion.110
  21.6 16.4 %all-reduce.2.cloned.1.call-done = bf16[1024,128]{1,0:T(8,128)(2,1)} async-done(((bf16[1024,128]{1,0:T(8,128)(2,1)}), bf16[1024,128]{1,0:T(8,128)(2,1)}) %all-reduce.2.cloned.1.call-update) | async-done | bytes 262160 | tf_op jit(solution)/shard_map/psum | solution.py:164
  38.0 1.7 fusion.82
  40.4 1.1 fusion.50
  41.6 0.9 fusion.28
  42.4 0.9 fusion.24
  43.3 0.9 fusion.22
  44.2 1.0 fusion.32
  50.4 4.2 %multiply_add_fusion = (f32[128,4,1,1024]{3,1,2,0:T(4,128)S(1)}, f32[128,4,1,1024]{3,1,2,0:T(4,128)S(1)}) fusion(f32[4,1024]{1,0:T(4,128)S(1)} %get-tuple-element.42, f32[128,1024]{1,0:T(8,128)S(1)} %get-tuple-element.103, f32[4,1024]{1,0:T(4,128)S(1)} %get-tuple-element.41, f32[128,1024]{1,0:T(8,128)S(1)} %get-tuple-element.109, ...), kind=kLoop, calls=%fused_computation.10 | loop fusion | flops 15728640 | bytes 8519680 | tf_op jit(solution)/shard_map/add | solution.py:122
  54.6 4.2 %multiply_add_fusion.1 = (f32[128,4,1,1024]{3,1,2,0:T(4,128)S(1)}, f32[128,4,1,1024]{3,1,2,0:T(4,128)S(1)}) fusion(f32[4,1024]{1,0:T(4,128)S(1)} %get-tuple-element.71, f32[128,1024]{1,0:T(8,128)S(1)} %get-tuple-element.112, f32[4,1024]{1,0:T(4,128)S(1)} %get-tuple-element.70, f32[128,1024]{1,0:T(8,128)S(1)} %get-tuple-element.114, ...), kind=kLoop, calls=%fused_computation.12 | loop fusion | flops 15728640 | bytes 8519680 | tf_op jit(solution)/shard_map/add | solution.py:122
  58.7 2.1 %fusion.1 = bf16[128,4,2,1024]{3,1,2,0:T(4,128)(2,1)S(1)} fusion(f32[128,4,1,1024]{3,1,2,0:T(4,128)S(1)} %get-tuple-element.98, f32[128,4,1,1024]{3,1,2,0:T(4,128)S(1)} %get-tuple-element.97, f32[128,4,1,1024]{3,1,2,0:T(4,128)S(1)} %get-tuple-element.96, f32[128,4,1,1024]{3,1,2,0:T(4,128)S(1)} %get-tuple-element.95, f32[128]{0:T(128)S(1)} %get-tuple-element.146, ...), kind=kLoop, calls=%fused_computation.4 | loop fusion | flops 6291456 | bytes 10486784 | tf_op jit(solution)/shard_map/convert_element_type | solution.py:188
  60.8 9.8 %gather_fusion = bf16[256,4,2,1024]{3,1,2,0:T(4,128)(2,1)} fusion(bf16[128,4,2,1024]{3,1,2,0:T(4,128)(2,1)S(1)} %fusion.1, s32[1024]{0:T(1024)S(1)} %pad_clamp_fusion.1), kind=kCustom, calls=%fused_computation | custom fusion | bytes 8389632 | tf_op jit(solution)/shard_map/jit(_take)/gather | solution.py:209
  70.6 7.1 %fusion.2 = bf16[32,8,4,2,1024]{4,1,0,3,2:T(8,128)(2,1)S(1)} fusion(bf16[256,4,2,1024]{3,1,2,0:T(4,128)(2,1)} %gather_fusion, pred[32,8]{1,0:T(8,128)(4,1)S(1)} %copy.25, bf16[32]{0:T(256)(128)(2,1)S(1)} %convert_element_type.86), kind=kLoop, calls=%fused_computation.7 | loop fusion | flops 4194304 | bytes 8388928 | tf_op jit(solution)/shard_map/mul | solution.py:212
  77.7 2.4 %copy.30 = bf16[32,8,4,2,1024]{4,1,3,2,0:T(8,128)(2,1)} copy(bf16[32,8,4,2,1024]{4,1,0,3,2:T(8,128)(2,1)S(1)} %fusion.2) | data formatting | bytes 8388608 | tf_op jit(solution)/shard_map/mul | solution.py:212
  80.5 21.2 %all-gather.1 = f32[8,1,128]{2,1,0:T(1,128)S(1)} all-gather(f32[1,1,128]{2,1,0:T(1,128)S(1)} %bitcast.239), channel_id=2, replica_groups=mesh['cell'=2,'ap'=8,'sc'=2] {'ap'}, dimensions={0}, use_global_device_ids=true | all-gather | bytes 4608 | tf_op jit(solution)/shard_map/all_gather | solution.py:180
  102.7 67.2 %reduce-scatter.2.cloned.1.call-done = bf16[4,8,4,2,1024]{4,1,3,2,0:T(8,128)(2,1)} async-done(((bf16[32,8,4,2,1024]{4,1,3,2,0:T(8,128)(2,1)}), bf16[4,8,4,2,1024]{4,1,3,2,0:T(8,128)(2,1)}) %reduce-scatter.2.cloned.1.call-update) | async-done | bytes 524304 | tf_op jit(solution)/shard_map/reduce_scatter | solution.py:211
  169.9 1.2 convert_divide_fusion
  171.1 1.8 copy.32
  (77 shorter events, 10.4 us)
Async XLA Ops:
  6.5 31.5 %all-reduce.2.cloned.1.call-start = ((), (), s32[]{:S(2)}) async-start(), calls=%async_computation.1 | async-start | bytes 524288 | tf_op jit(solution)/shard_map/psum | solution.py:164
  14.7 4.5 %copy-start.4 = (s32[128]{0:T(128)S(1)}, s32[128]{0:T(128)}, u32[]{:S(2)}) copy-start(s32[128]{0:T(128)} %param.13) | copy-start | bytes 1540
  14.7 4.7 %copy-start.2 = (s32[16,1]{0,1:T(1,128)S(1)}, s32[16,1]{0,1:T(1,128)}, u32[]{:S(2)}) copy-start(s32[16,1]{0,1:T(1,128)} %param.15) | copy-start | bytes 196
  14.7 5.6 %copy-start.7 = (f32[128]{0:T(128)S(1)}, f32[128]{0:T(128)}, u32[]{:S(2)}) copy-start(f32[128]{0:T(128)} %param.10) | copy-start | bytes 1540
  14.7 5.6 %copy-start.3 = (f32[2]{0:T(128)S(1)}, f32[2]{0:T(128)}, u32[]{:S(2)}) copy-start(f32[2]{0:T(128)} %param.11) | copy-start | bytes 28
  14.7 6.3 %copy-start.5 = (s32[16,16]{1,0:T(8,128)S(1)}, s32[16,16]{1,0:T(8,128)}, u32[]{:S(2)}) copy-start(s32[16,16]{1,0:T(8,128)} %param.14) | copy-start | bytes 3076
  14.7 6.3 %copy-start.6 = (f32[2,128]{1,0:T(2,128)S(1)}, f32[2,128]{1,0:T(2,128)}, u32[]{:S(2)}) copy-start(f32[2,128]{1,0:T(2,128)} %param.12) | copy-start | bytes 3076
  14.8 6.8 %copy-start.1 = (bf16[2,4,2,4,1024]{4,3,2,1,0:T(4,128)(2,1)S(1)}, bf16[2,4,2,4,1024]{4,3,2,1,0:T(4,128)(2,1)}, u32[]{:S(2)}) copy-start(bf16[2,4,2,4,1024]{4,3,2,1,0:T(4,128)(2,1)} %param.9) | copy-start | bytes 393220
  16.9 153.0 %reduce-scatter.2.cloned.1.call-start = ((), (), s32[]{:S(2)}) async-start(), calls=%async_computation.2 | async-start | bytes 4718592 | tf_op jit(solution)/shard_map/reduce_scatter | solution.py:211
  38.0 1.7 copy-start
Sparse Core Ops, SparseCore 0:
  17.0 20.9 all-reduce.1
  80.3 89.5 reduce-scatter.1
